TPU v7x, 32 devices: a whole 2x2x4 slice. The times are simulated.
32 devices in a mesh: groups: 2 (over y), ctx: 8 (over z, x), kvh: 2 (over core).
Axes of the slice: x: 2, y: 2, z: 4, core: 2. Of those that a mesh axis runs over, the one named last changes fastest.
Arguments:
- queries: bfloat16 [2048, 4, 8, 128], P(('groups', 'ctx'), 'kvh'), parts along dimension 0, may hold values from -120 to 120
- keys: bfloat16 [2048, 4, 128], P(('groups', 'ctx'), 'kvh'), parts along dimension 0, may hold values from -8 to 8
- values: bfloat16 [2048, 4, 128], P(('groups', 'ctx'), 'kvh'), parts along dimension 0, may hold values from -6 to 6
- seq_lengths: int32 [8], P('groups'), parts along dimension 0, may hold values from 1 to 768, 1024 in all
Outputs:
- attended: bfloat16 [2048, 4, 8, 128], P(('groups', 'ctx'), 'kvh'), parts along dimension 0
There are 2 independent parts, one for each index of `groups`. A program takes and returns all parts, laid end to end along the dimension named above; each array names one. Nothing has to cross between parts.
Inputs may be any that keep to these rules, and one draw needn't show every extreme that they name: `seq_lengths`: sum to 1024; the longest is exactly 768.
All inputs are finite; a program needn't handle non-finite values.
Results may differ from a plain program's by a relative error of at most 0.005.
Values may be sent and summed in bfloat16 or wider, within the bound.
No kernel may reach another device: no remote copies, remote signals or barrier semaphores. Data moves between devices by JAX's collectives and lax.ppermute only.
A program may use at most 64 MiB of HBM per device.

v0:
```python
import math
import jax
import jax.numpy as jnp
from jax import lax
from jax.sharding import PartitionSpec as P


def seq_index(positions, starts):
    return jnp.sum((positions[:, None] >= starts[None, :]).astype(jnp.int32), axis=1)


def attend(work_queries, work_pos, keys, values, starts):
    row_count, local_heads, group_size, head_size = work_queries.shape
    score_scale = 1.0 / math.sqrt(head_size)
    query_seq = seq_index(work_pos, starts)
    last_pos = jnp.max(work_pos)
    first_needed = jnp.min(starts[query_seq - 1])
    initial = (
        jnp.full((row_count, local_heads, group_size), -1e30, jnp.float32),
        jnp.zeros((row_count, local_heads, group_size), jnp.float32),
        jnp.zeros((row_count, local_heads, group_size, head_size), jnp.float32),
    )
    first_row = jnp.int32(0)
    key_piece = lax.all_gather(keys, "ctx", axis=0, tiled=True)
    value_piece = lax.all_gather(values, "ctx", axis=0, tiled=True)
    piece_rows = key_piece.shape[0]
    tile_rows = math.gcd(piece_rows, 512)
    tile_count = piece_rows // tile_rows

    def one_tile(running, inputs):
        key_tile, value_tile, offset = inputs
        key_pos = offset + jnp.arange(tile_rows, dtype=jnp.int32)
        key_seq = seq_index(key_pos, starts)
        allowed = (key_seq[None, :] == query_seq[:, None]) & (key_pos[None, :] <= work_pos[:, None])
        scores = (
            jnp.einsum("rkgd,tkd->rkgt", work_queries, key_tile, preferred_element_type=jnp.float32)
            * score_scale
        )
        scores = jnp.where(allowed[:, None, None, :], scores, -jnp.inf)
        running_max, running_sum, weighted = running
        new_max = jnp.maximum(running_max, jnp.max(scores, axis=3))
        factor = jnp.exp(running_max - new_max)
        weights = jnp.exp(scores - new_max[..., None])
        new_sum = running_sum * factor + jnp.sum(weights, axis=3)
        product = jnp.einsum(
            "rkgt,tkd->rkgd",
            weights.astype(jnp.bfloat16),
            value_tile,
            preferred_element_type=jnp.float32,
        )
        return ((new_max, new_sum, weighted * factor[..., None] + product), None)

    key_tiles = key_piece.reshape(tile_count, tile_rows, local_heads, head_size)
    value_tiles = value_piece.reshape(tile_count, tile_rows, local_heads, head_size)
    offsets = jnp.arange(tile_count, dtype=jnp.int32) * tile_rows

    def run_tiles(running):
        return lax.scan(one_tile, running, (key_tiles, value_tiles, offsets))[0]

    visible = (first_row <= last_pos) & (first_row + piece_rows - 1 >= first_needed)
    running_max, running_sum, weighted = lax.cond(
        visible, run_tiles, lambda running: running, initial
    )
    return (weighted / running_sum[..., None]).astype(jnp.bfloat16)


def on_device(queries, keys, values, seq_lengths):
    row_count = queries.shape[0]
    my_index = lax.axis_index("ctx")
    starts = jnp.cumsum(seq_lengths) - seq_lengths
    own_pos = my_index * row_count + jnp.arange(row_count, dtype=jnp.int32)
    return attend(queries, own_pos, keys, values, starts)


def solution(mesh):
    placed = (
        P(("groups", "ctx"), "kvh", None, None),
        P(("groups", "ctx"), "kvh", None),
        P(("groups", "ctx"), "kvh", None),
        P("groups"),
    )
    return jax.shard_map(
        on_device,
        mesh=mesh,
        in_specs=placed,
        out_specs=P(("groups", "ctx"), "kvh", None, None),
        check_vma=False,
    )
```

profile of v0, /device:TPU:0, one launch (start us, length us, event | category | flops | bytes accessed | tf_op | source)
XLA Modules:
  0.0 96.8 jit_solution(3941921183998855034)
XLA Ops:
  0.0 0.8 reduce-window.9
  0.8 0.7 bitcast_subtract_fusion
  1.5 0.1 convert_reduce_fusion.1
  1.6 0.6 fusion.27
  2.2 3.2 %fusion.25 = s32[]{:T(128)} fusion(s32[128]{0:T(128)S(1)} %convert_reduce_fusion.1, s32[]{:T(128)} %bitcast.6, s32[]{:T(128)} %bitcast.7, s32[]{:T(128)} %bitcast.9, s32[]{:T(128)} %bitcast.8), kind=kLoop, calls=%fused_computation.36 | loop fusion | flops 1407 | bytes 532 | tf_op jit(solution)/shard_map/reduce_min | solution.py:17
  6.1 0.6 fusion.26
  7.3 0.9 copy.21
  8.2 33.0 %all_gather.6 = bf16[1024,2,128]{2,0,1:T(8,128)(2,1)S(1)} all-gather(bf16[128,2,128]{2,0,1:T(8,128)(2,1)S(1)} %copy.21), channel_id=1, replica_groups=mesh['groups'=2,'ctx'=8,'kvh'=2] {'ctx'}, dimensions={0}, use_global_device_ids=true | all-gather | bytes 589824 | tf_op jit(solution)/shard_map/all_gather | solution.py:24
  41.2 0.8 copy.22
  42.1 31.3 %all_gather.7 = bf16[1024,2,128]{2,0,1:T(8,128)(2,1)S(1)} all-gather(bf16[128,2,128]{2,0,1:T(8,128)(2,1)S(1)} %copy.22), channel_id=1, replica_groups=mesh['groups'=2,'ctx'=8,'kvh'=2] {'ctx'}, dimensions={0}, use_global_device_ids=true | all-gather | bytes 589824 | tf_op jit(solution)/shard_map/all_gather | solution.py:25
  73.4 21.4 %conditional.1 = (f32[128,2,8]{0,2,1:T(8,128)}, f32[128,2,8,128]{3,2,1,0:T(8,128)S(1)}) conditional(s32[]{:T(128)} %convert_element_type.16, () %tuple.20, (bf16[1024,2,128]{2,0,1:T(8,128)(2,1)S(1)}, bf16[1024,2,128]{2,0,1:T(8,128)(2,1)S(1)}, s32[2]{0:T(128)S(1)}, s32[4]{0:T(128)S(1)}, s32[128]{0:T(128)S(1)}, /*index=5*/s32[128]{0:T(128)S(1)}, ...), branch_computations={%region_4.5_spmd, %region_5.11_spmd} | conditional | flops 549404672 | bytes 36056412 | solution.py:61
  73.4 1.2 %copy.23 = bf16[128,2,8,128]{3,0,2,1:T(8,128)(2,1)S(1)} copy(bf16[128,2,8,128]{3,2,1,0:T(8,128)(2,1)} %get-tuple-element.187) | data formatting | bytes 1048576 | tf_op jit(solution)/shard_map
  74.6 19.7 %while.18 = (s32[]{:T(128)}, f32[128,2,8]{0,2,1:T(8,128)S(1)}, f32[128,2,8]{0,2,1:T(8,128)}, f32[128,2,8,128]{0,3,2,1:T(8,128)S(1)}, s32[2]{0:T(128)S(1)}, /*ind...) while((s32[]{:T(128)}, f32[128,2,8]{0,2,1:T(8,128)S(1)}, ...), condition=%wide.region_10.10_spmd.clone, body=%wide.region_6.9_spmd.clone.sunk | while | flops 549404672 | bytes 32910540 | solution.py:58
  74.6 0.7 dynamic_slice.29
  75.3 0.7 iota_add_fusion.3
  76.0 0.1 convert_reduce_fusion.3
  76.0 0.2 compare_and_fusion.2
  76.3 2.6 %fusion.39 = (f32[128,2,8]{0,2,1:T(8,128)S(1)}, f32[2,512,128,8]{2,1,3,0:T(8,128)}) fusion(pred[128,512]{0,1:T(8,128)(4,1)S(1)} %compare_and_fusion.2, bf16[128,2,8,128]{3,0,2,1:T(8,128)(2,1)S(1)} %get-tuple-element.329, bf16[2,512,2,128]{3,1,0,2:T(8,128)(2,1)S(1)} %get-tuple-element.328, s32[]{:T(128)} %get-tuple-element.307), kind=kOutput, calls=%fused_computation.4.clone.1 | convolution fusion | flops 271579136 | bytes 5054468 | tf_op jit(solution)/shard_map/cond/branch_1_fun/while/body/eval_jaxpr/rkgd,tkd->rkgt/dot_general | solution.py:36
  78.9 0.0 copy-start
  78.9 3.2 %fusion.40 = f32[128,2,8]{0,2,1:T(8,128)S(1)} fusion(f32[2,512,128,8]{2,1,3,0:T(8,128)} %get-tuple-element.291, f32[128,2,8]{0,2,1:T(8,128)S(1)} %select_maximum_fusion.2, pred[128,512]{0,1:T(8,128)(4,1)S(1)} %compare_and_fusion.2), kind=kLoop, calls=%fused_computation.3.clone.1 | loop fusion | flops 4192256 | bytes 4276224 | tf_op jit(solution)/shard_map/cond/branch_1_fun/while/body/eval_jaxpr/reduce_sum | solution.py:44
  82.1 0.6 fusion.41
  82.7 0.0 copy-done
  82.7 1.3 %fusion.42 = f32[128,2,8,128]{0,3,2,1:T(8,128)S(1)} fusion(f32[2,512,128,8]{2,1,3,0:T(8,128)S(1)} %copy-done, f32[128,2,8]{0,2,1:T(8,128)S(1)} %select_maximum_fusion.2, pred[128,512]{0,1:T(8,128)(4,1)S(1)} %compare_and_fusion.2, f32[128,2,8,128]{0,3,2,1:T(8,128)S(1)} %get-tuple-element.310, f32[128,2,8]{0,2,1:T(8,128)S(1)} %get-tuple-element.293, ...), kind=kOutput, calls=%fused_computation.11.clone.1 | convolution fusion | flops 273416192 | bytes 6635525 | tf_op jit(solution)/shard_map/cond/branch_1_fun/while/body/eval_jaxpr/rkgt,tkd->rkgd/dot_general | solution.py:45
  84.1 0.7 dynamic_slice.29
  84.8 0.7 iota_add_fusion.3
  85.5 0.1 convert_reduce_fusion.3
  85.5 0.2 compare_and_fusion.2
  85.8 2.6 %fusion.39 = (f32[128,2,8]{0,2,1:T(8,128)S(1)}, f32[2,512,128,8]{2,1,3,0:T(8,128)}) fusion(pred[128,512]{0,1:T(8,128)(4,1)S(1)} %compare_and_fusion.2, bf16[128,2,8,128]{3,0,2,1:T(8,128)(2,1)S(1)} %get-tuple-element.329, bf16[2,512,2,128]{3,1,0,2:T(8,128)(2,1)S(1)} %get-tuple-element.328, s32[]{:T(128)} %get-tuple-element.307), kind=kOutput, calls=%fused_computation.4.clone.1 | convolution fusion | flops 271579136 | bytes 5054468 | tf_op jit(solution)/shard_map/cond/branch_1_fun/while/body/eval_jaxpr/rkgd,tkd->rkgt/dot_general | solution.py:36
  88.4 0.0 copy-start
  88.4 3.2 %fusion.40 = f32[128,2,8]{0,2,1:T(8,128)S(1)} fusion(f32[2,512,128,8]{2,1,3,0:T(8,128)} %get-tuple-element.291, f32[128,2,8]{0,2,1:T(8,128)S(1)} %select_maximum_fusion.2, pred[128,512]{0,1:T(8,128)(4,1)S(1)} %compare_and_fusion.2), kind=kLoop, calls=%fused_computation.3.clone.1 | loop fusion | flops 4192256 | bytes 4276224 | tf_op jit(solution)/shard_map/cond/branch_1_fun/while/body/eval_jaxpr/reduce_sum | solution.py:44
  91.6 1.3 %fusion.41 = (f32[128,2,8]{0,2,1:T(8,128)}, f32[128,2,8]{0,2,1:T(8,128)S(1)}) fusion(f32[128,2,8]{0,2,1:T(8,128)S(1)} %fusion.40, f32[128,2,8]{0,2,1:T(8,128)} %get-tuple-element.309, pred[]{:T(512)S(6)} %compare.26, f32[128,2,8]{0,2,1:T(8,128)S(1)} %select_maximum_fusion.2, f32[128,2,8]{0,2,1:T(8,128)S(1)} %get-tuple-element.308), kind=kLoop, calls=%fused_computation.20.clone.1 | loop fusion | flops 10240 | bytes 49153 | tf_op jit(solution)/shard_map/cond/branch_1_fun/while/body/eval_jaxpr/add | solution.py:44
  92.9 0.0 copy-done
  92.9 1.3 %fusion.42 = f32[128,2,8,128]{0,3,2,1:T(8,128)S(1)} fusion(f32[2,512,128,8]{2,1,3,0:T(8,128)S(1)} %copy-done, f32[128,2,8]{0,2,1:T(8,128)S(1)} %select_maximum_fusion.2, pred[128,512]{0,1:T(8,128)(4,1)S(1)} %compare_and_fusion.2, f32[128,2,8,128]{0,3,2,1:T(8,128)S(1)} %get-tuple-element.310, f32[128,2,8]{0,2,1:T(8,128)S(1)} %get-tuple-element.293, ...), kind=kOutput, calls=%fused_computation.11.clone.1 | convolution fusion | flops 273416192 | bytes 6635525 | tf_op jit(solution)/shard_map/cond/branch_1_fun/while/body/eval_jaxpr/rkgt,tkd->rkgd/dot_general | solution.py:45
  94.3 0.5 copy.30
  94.8 0.8 copy.24
  95.6 1.1 %divide_convert_fusion = bf16[128,2,8,128]{3,2,1,0:T(8,128)(2,1)} fusion(f32[128,2,8,128]{3,2,1,0:T(8,128)S(1)} %get-tuple-element.188, f32[128,2,8]{2,1,0:T(2,128)S(1)} %copy.24), kind=kLoop, calls=%fused_computation.30 | loop fusion | flops 524288 | bytes 1581056 | tf_op jit(solution)/shard_map/convert_element_type | solution.py:64
  (10 shorter events, 0.0 us)
Async XLA Ops:
  78.9 3.8 %copy-start = (f32[2,512,128,8]{2,1,3,0:T(8,128)S(1)}, f32[2,512,128,8]{2,1,3,0:T(8,128)}, u32[]{:S(2)}) copy-start(f32[2,512,128,8]{2,1,3,0:T(8,128)} %get-tuple-element.291) | copy-start | bytes 12582916 | tf_op jit(solution)/shard_map/cond/branch_1_fun/while
  88.4 4.5 %copy-start = (f32[2,512,128,8]{2,1,3,0:T(8,128)S(1)}, f32[2,512,128,8]{2,1,3,0:T(8,128)}, u32[]{:S(2)}) copy-start(f32[2,512,128,8]{2,1,3,0:T(8,128)} %get-tuple-element.291) | copy-start | bytes 12582916 | tf_op jit(solution)/shard_map/cond/branch_1_fun/while
where the time goes:
time: 97.2 us; the launch traced here: 96.8 us
  blocking collectives  64.3 us (66%)
  other arithmetic  16.9 us (17%)
  matrix products  7.91 us (8%)
  local copies, waits for them, and re-layouts  6.19 us (6%)
  between operations  1.32 us (1%)
    all_gather x1, blocking collectives, attend(): key_piece = lax.all_gather(keys, 'ctx', axis=0, tiled=True)  33 us
    all_gather x1, blocking collectives, attend(): value_piece = lax.all_gather(values, 'ctx', axis=0, tiled=True)  31.3 us
    reduce_sum x2, other arithmetic, one_tile(): new_sum = running_sum * factor + jnp.sum(weights, axis=3)  6.42 us
    dot_general x2, matrix products, one_tile(): jnp.einsum('rkgd,tkd->rkgt', work_queries, key_tile, preferred_element_ty...  5.28 us
    reduce_min x1, other arithmetic, attend(): first_needed = jnp.min(starts[query_seq - 1])  3.22 us
    dot_general x2, matrix products, one_tile(): jnp.einsum('rkgt,tkd->rkgd', weights.astype(jnp.bfloat16), value_tile, pr...  2.64 us

commit v1 on v0

--- a/solution.py
+++ b/solution.py
@@ -21,7 +21,14 @@
         jnp.zeros((row_count, local_heads, group_size, head_size), jnp.float32),
     )
     first_row = jnp.int32(0)
-    key_piece = lax.all_gather(keys, "ctx", axis=0, tiled=True)
+    ways, here, step = (lax.axis_size("ctx"), lax.axis_index("ctx"), keys.shape[0])
+    line, have = (keys, 1)
+    while have < ways:
+        line = jnp.concatenate(
+            [line, lax.ppermute(line, "ctx", [(d, (d - have) % ways) for d in range(ways)])], axis=0
+        )
+        have = 2 * have
+    key_piece = jnp.roll(line, here * step, axis=0)
     value_piece = lax.all_gather(values, "ctx", axis=0, tiled=True)
     piece_rows = key_piece.shape[0]
     tile_rows = math.gcd(piece_rows, 512)

time: 97.2 us -> 82.1 us (0.84)
  blocking collectives: 64.3 us -> 31.5 us
  waiting for transfers between devices: 0 us -> 8.97 us
  starting transfers between devices: 0 us -> 7.42 us
  local copies, waits for them, and re-layouts: 6.19 us -> 7.34 us
    all_gather x1 -> x0, blocking collectives: 33 us -> none  [attend(): key_piece = lax.all_gather(keys, 'ctx', axis=0, tiled=True)]
    ppermute x0 -> x3, waiting for transfers between devices: none -> 8.97 us  [attend(): lax.ppermute(line, 'ctx', [(d, (d - have) % ways) for d in range(ways)])]
    ppermute x0 -> x3, starting transfers between devices: none -> 7.42 us  [attend(): lax.ppermute(line, 'ctx', [(d, (d - have) % ways) for d in range(ways)])]
    unnamed x2 -> x8, local copies, waits for them, and re-layouts: 1.7 us -> 2.67 us
  transfers between devices with their start and end apart: 0 -> 3, of which waited for: 0 -> 2; matrix products, arithmetic and copies ran while one was open for 0% -> 8% of each run, Pallas kernels for 0% -> 0%
where the time goes in v1:
time: 82.1 us; the launch traced here: 81.7 us
  blocking collectives  31.5 us (38%)
  other arithmetic  16.9 us (21%)
  waiting for transfers between devices  8.97 us (11%)
  matrix products  7.91 us (10%)
  starting transfers between devices  7.42 us (9%)
  local copies, waits for them, and re-layouts  7.34 us (9%)
  between operations  1.37 us (2%)
    all_gather x1, blocking collectives, attend(): value_piece = lax.all_gather(values, 'ctx', axis=0, tiled=True)  31.5 us
    ppermute x3, waiting for transfers between devices, attend(): lax.ppermute(line, 'ctx', [(d, (d - have) % ways) for d in range(ways)])  8.97 us
    ppermute x3, starting transfers between devices, attend(): lax.ppermute(line, 'ctx', [(d, (d - have) % ways) for d in range(ways)])  7.42 us
    reduce_sum x2, other arithmetic, one_tile(): new_sum = running_sum * factor + jnp.sum(weights, axis=3)  6.42 us
    dot_general x2, matrix products, one_tile(): jnp.einsum('rkgd,tkd->rkgt', work_queries, key_tile, preferred_element_ty...  5.27 us
    reduce_min x1, other arithmetic, attend(): first_needed = jnp.min(starts[query_seq - 1])  3.22 us
    unnamed x8, local copies, waits for them, and re-layouts  2.67 us
    dot_general x2, matrix products, one_tile(): jnp.einsum('rkgt,tkd->rkgd', weights.astype(jnp.bfloat16), value_tile, pr...  2.64 us
  transfers between devices with their start and end apart: 3, of which 2 were waited for; matrix products, arithmetic and copies ran while one was open for 8% of the time, Pallas kernels for 0%

profile of v1, /device:TPU:0, one launch (start us, length us, event | category | flops | bytes accessed | tf_op | source)
XLA Modules:
  0.0 81.7 jit_solution(14678608644459794908)
XLA Ops:
  0.0 0.9 %fusion.26 = (bf16[128,2,128]{2,0,1:T(8,128)(2,1)S(1)}, bf16[2048,2,128]{2,0,1:T(8,128)(2,1)S(1)}) fusion(bf16[128,2,128]{2,1,0:T(2,128)(2,1)} %param.9), kind=kLoop, calls=%fused_computation.51 | loop fusion | bytes 196608 | tf_op args[1]
  0.9 6.0 %collective-permute-start = (bf16[128,2,128]{2,0,1:T(8,128)(2,1)S(1)}, bf16[128,2,128]{2,0,1:T(8,128)(2,1)S(1)}, u32[]{:S(2)}, u32[]{:S(2)}) collective-permute-start(bf16[128,2,128]{2,0,1:T(8,128)(2,1)S(1)} %get-tuple-element.329), channel_id=1, source_target_pairs={{0,14},{2,0},{4,2},{6,4},{8,6},{10,8},{12,10},{14,12},{1,15},{3,1}... | collective-permute-start | bytes 196616 | tf_op jit(solution)/shard_map/ppermute | solution.py:28
  6.9 0.8 %reduce-window.9 = s32[4,1]{0,1:T(1,128)S(1)} reduce-window(s32[4,1]{0,1:T(1,128)} %bitcast.67, s32[]{:T(128)} %constant.90.clone.1), window={size=4x1 pad=3_0x0_0}, to_apply=%region_1.2 | reduce-window | flops 12 | bytes 36 | tf_op jit(solution)/shard_map/reduce-window.4
  7.7 0.7 bitcast_subtract_fusion
  8.4 0.8 %copy.30 = bf16[128,2,128]{2,0,1:T(8,128)(2,1)S(1)} copy(bf16[128,2,128]{2,1,0:T(2,128)(2,1)} %param.10) | data formatting | bytes 131072 | tf_op args[2]
  9.2 31.5 %all_gather.3 = bf16[1024,2,128]{2,0,1:T(8,128)(2,1)S(1)} all-gather(bf16[128,2,128]{2,0,1:T(8,128)(2,1)S(1)} %copy.30), channel_id=1, replica_groups=mesh['groups'=2,'ctx'=8,'kvh'=2] {'ctx'}, dimensions={0}, use_global_device_ids=true | all-gather | bytes 589824 | tf_op jit(solution)/shard_map/all_gather | solution.py:32
  40.7 0.6 fusion.27
  41.4 0.0 collective-permute-done
  41.4 0.6 collective-permute-start.1
  42.0 0.1 convert_reduce_fusion.1
  42.1 4.8 %collective-permute-done.1 = bf16[256,2,128]{2,0,1:T(8,128)(2,1)S(1)} collective-permute-done((bf16[256,2,128]{2,0,1:T(8,128)(2,1)S(1)}, bf16[256,2,128]{2,0,1:T(8,128)(2,1)S(1)}, u32[]{:S(2)}, u32[]{:S(2)}) %collective-permute-start.1) | collective-permute-done | bytes 131104 | tf_op jit(solution)/shard_map/ppermute | solution.py:28
  46.9 0.8 collective-permute-start.2
  47.7 3.2 %fusion.25 = s32[]{:T(128)} fusion(s32[128]{0:T(128)S(1)} %convert_reduce_fusion.1, s32[]{:T(128)} %bitcast.6, s32[]{:T(128)} %bitcast.7, s32[]{:T(128)} %bitcast.9, s32[]{:T(128)} %bitcast.8), kind=kLoop, calls=%fused_computation.49 | loop fusion | flops 1407 | bytes 532 | tf_op jit(solution)/shard_map/reduce_min | solution.py:17
  50.9 0.6 add_reduce_fusion
  52.9 4.2 %collective-permute-done.2 = bf16[512,2,128]{2,0,1:T(8,128)(2,1)S(1)} collective-permute-done((bf16[512,2,128]{2,0,1:T(8,128)(2,1)S(1)}, bf16[512,2,128]{2,0,1:T(8,128)(2,1)S(1)}, u32[]{:S(2)}, u32[]{:S(2)}) %collective-permute-start.2) | collective-permute-done | bytes 262176 | tf_op jit(solution)/shard_map/ppermute | solution.py:28
  57.1 0.9 %constant_dynamic-update-slice_fusion.3 = bf16[2048,2,128]{2,0,1:T(8,128)(2,1)S(1)} fusion(bf16[2048,2,128]{2,0,1:T(8,128)(2,1)S(1)} %constant_dynamic-update-slice_fusion.4, bf16[128,2,128]{2,1,0:T(2,128)(2,1)} %param.9), kind=kLoop, calls=%fused_computation.37 | loop fusion | bytes 131072
  58.1 21.6 %conditional.1 = (f32[128,2,8]{0,2,1:T(8,128)}, f32[128,2,8,128]{3,2,1,0:T(8,128)S(1)}) conditional(s32[]{:T(128)} %convert_element_type.16, () %tuple.32, (s32[]{:T(128)}, s32[]{:T(128)}, bf16[2048,2,128]{2,0,1:T(8,128)(2,1)S(1)}, bf16[1024,2,128]{2,0,1:T(8,128)(2,1)S(1)}, s32[2]{0:T(128)S(1)}, /*index=5*/s32[4]{0:T(128)S(1)}, s32[128]{0:T(128)S(1)}, ...), branch_computations={%region_4.5_spmd, %region_5.11_spmd} | conditional | flops 549404672 | bytes 37105148 | solution.py:68
  58.1 0.1 constant_dynamic-slice_fusion
  58.3 1.2 %copy.31 = bf16[128,2,8,128]{3,0,2,1:T(8,128)(2,1)S(1)} copy(bf16[128,2,8,128]{3,2,1,0:T(8,128)(2,1)} %get-tuple-element.296) | data formatting | bytes 1048576 | tf_op jit(solution)/shard_map
  59.5 19.7 %while.26 = (s32[]{:T(128)}, f32[128,2,8]{0,2,1:T(8,128)S(1)}, f32[128,2,8]{0,2,1:T(8,128)}, f32[128,2,8,128]{0,3,2,1:T(8,128)S(1)}, s32[2]{0:T(128)S(1)}, /*ind...) while((s32[]{:T(128)}, f32[128,2,8]{0,2,1:T(8,128)S(1)}, ...), condition=%wide.region_10.10_spmd.clone, body=%wide.region_6.9_spmd.clone.sunk | while | flops 549404672 | bytes 32910540 | solution.py:65
  59.5 0.7 dynamic_slice.40
  60.1 0.7 iota_add_fusion.3
  60.8 0.1 convert_reduce_fusion.3
  60.9 0.2 compare_and_fusion.2
  61.1 2.6 %fusion.39 = (f32[128,2,8]{0,2,1:T(8,128)S(1)}, f32[2,512,128,8]{2,1,3,0:T(8,128)}) fusion(pred[128,512]{0,1:T(8,128)(4,1)S(1)} %compare_and_fusion.2, bf16[128,2,8,128]{3,0,2,1:T(8,128)(2,1)S(1)} %get-tuple-element.445, bf16[2,512,2,128]{3,1,0,2:T(8,128)(2,1)S(1)} %get-tuple-element.444, s32[]{:T(128)} %get-tuple-element.423), kind=kOutput, calls=%fused_computation.4.clone.1 | convolution fusion | flops 271579136 | bytes 5054468 | tf_op jit(solution)/shard_map/cond/branch_1_fun/while/body/eval_jaxpr/rkgd,tkd->rkgt/dot_general | solution.py:43
  63.8 0.0 copy-start
  63.8 3.2 %fusion.40 = f32[128,2,8]{0,2,1:T(8,128)S(1)} fusion(f32[2,512,128,8]{2,1,3,0:T(8,128)} %get-tuple-element.407, f32[128,2,8]{0,2,1:T(8,128)S(1)} %select_maximum_fusion.2, pred[128,512]{0,1:T(8,128)(4,1)S(1)} %compare_and_fusion.2), kind=kLoop, calls=%fused_computation.3.clone.1 | loop fusion | flops 4192256 | bytes 4276224 | tf_op jit(solution)/shard_map/cond/branch_1_fun/while/body/eval_jaxpr/reduce_sum | solution.py:51
  67.0 0.6 fusion.41
  67.6 0.0 copy-done
  67.6 1.3 %fusion.42 = f32[128,2,8,128]{0,3,2,1:T(8,128)S(1)} fusion(f32[2,512,128,8]{2,1,3,0:T(8,128)S(1)} %copy-done, f32[128,2,8]{0,2,1:T(8,128)S(1)} %select_maximum_fusion.2, pred[128,512]{0,1:T(8,128)(4,1)S(1)} %compare_and_fusion.2, f32[128,2,8,128]{0,3,2,1:T(8,128)S(1)} %get-tuple-element.426, f32[128,2,8]{0,2,1:T(8,128)S(1)} %get-tuple-element.409, ...), kind=kOutput, calls=%fused_computation.11.clone.1 | convolution fusion | flops 273416192 | bytes 6635525 | tf_op jit(solution)/shard_map/cond/branch_1_fun/while/body/eval_jaxpr/rkgt,tkd->rkgd/dot_general | solution.py:52
  69.0 0.7 dynamic_slice.40
  69.6 0.7 iota_add_fusion.3
  70.3 0.1 convert_reduce_fusion.3
  70.4 0.2 compare_and_fusion.2
  70.6 2.6 %fusion.39 = (f32[128,2,8]{0,2,1:T(8,128)S(1)}, f32[2,512,128,8]{2,1,3,0:T(8,128)}) fusion(pred[128,512]{0,1:T(8,128)(4,1)S(1)} %compare_and_fusion.2, bf16[128,2,8,128]{3,0,2,1:T(8,128)(2,1)S(1)} %get-tuple-element.445, bf16[2,512,2,128]{3,1,0,2:T(8,128)(2,1)S(1)} %get-tuple-element.444, s32[]{:T(128)} %get-tuple-element.423), kind=kOutput, calls=%fused_computation.4.clone.1 | convolution fusion | flops 271579136 | bytes 5054468 | tf_op jit(solution)/shard_map/cond/branch_1_fun/while/body/eval_jaxpr/rkgd,tkd->rkgt/dot_general | solution.py:43
  73.3 0.0 copy-start
  73.3 3.2 %fusion.40 = f32[128,2,8]{0,2,1:T(8,128)S(1)} fusion(f32[2,512,128,8]{2,1,3,0:T(8,128)} %get-tuple-element.407, f32[128,2,8]{0,2,1:T(8,128)S(1)} %select_maximum_fusion.2, pred[128,512]{0,1:T(8,128)(4,1)S(1)} %compare_and_fusion.2), kind=kLoop, calls=%fused_computation.3.clone.1 | loop fusion | flops 4192256 | bytes 4276224 | tf_op jit(solution)/shard_map/cond/branch_1_fun/while/body/eval_jaxpr/reduce_sum | solution.py:51
  76.5 1.3 %fusion.41 = (f32[128,2,8]{0,2,1:T(8,128)}, f32[128,2,8]{0,2,1:T(8,128)S(1)}) fusion(f32[128,2,8]{0,2,1:T(8,128)S(1)} %fusion.40, f32[128,2,8]{0,2,1:T(8,128)} %get-tuple-element.425, pred[]{:T(512)S(6)} %compare.27, f32[128,2,8]{0,2,1:T(8,128)S(1)} %select_maximum_fusion.2, f32[128,2,8]{0,2,1:T(8,128)S(1)} %get-tuple-element.424), kind=kLoop, calls=%fused_computation.20.clone.1 | loop fusion | flops 10240 | bytes 49153 | tf_op jit(solution)/shard_map/cond/branch_1_fun/while/body/eval_jaxpr/add | solution.py:51
  77.8 0.0 copy-done
  77.8 1.3 %fusion.42 = f32[128,2,8,128]{0,3,2,1:T(8,128)S(1)} fusion(f32[2,512,128,8]{2,1,3,0:T(8,128)S(1)} %copy-done, f32[128,2,8]{0,2,1:T(8,128)S(1)} %select_maximum_fusion.2, pred[128,512]{0,1:T(8,128)(4,1)S(1)} %compare_and_fusion.2, f32[128,2,8,128]{0,3,2,1:T(8,128)S(1)} %get-tuple-element.426, f32[128,2,8]{0,2,1:T(8,128)S(1)} %get-tuple-element.409, ...), kind=kOutput, calls=%fused_computation.11.clone.1 | convolution fusion | flops 273416192 | bytes 6635525 | tf_op jit(solution)/shard_map/cond/branch_1_fun/while/body/eval_jaxpr/rkgt,tkd->rkgd/dot_general | solution.py:52
  79.2 0.5 copy.38
  79.7 0.8 %copy.32 = f32[128,2,8]{2,1,0:T(2,128)S(1)} copy(f32[128,2,8]{0,2,1:T(8,128)} %get-tuple-element.197) | data formatting | bytes 16384 | tf_op jit(solution)/shard_map/cond | solution.py:68
  80.5 1.1 %divide_convert_fusion = bf16[128,2,8,128]{3,2,1,0:T(8,128)(2,1)} fusion(f32[128,2,8,128]{3,2,1,0:T(8,128)S(1)} %get-tuple-element.300, f32[128,2,8]{2,1,0:T(2,128)S(1)} %copy.32), kind=kLoop, calls=%fused_computation.31 | loop fusion | flops 524288 | bytes 1581056 | tf_op jit(solution)/shard_map/convert_element_type | solution.py:71
  (18 shorter events, 0.2 us)
Async XLA Ops:
  0.9 40.5 %collective-permute-start = (bf16[128,2,128]{2,0,1:T(8,128)(2,1)S(1)}, bf16[128,2,128]{2,0,1:T(8,128)(2,1)S(1)}, u32[]{:S(2)}, u32[]{:S(2)}) collective-permute-start(bf16[128,2,128]{2,0,1:T(8,128)(2,1)S(1)} %get-tuple-element.329), channel_id=1, source_target_pairs={{0,14},{2,0},{4,2},{6,4},{8,6},{10,8},{12,10},{14,12},{1,15},{3,1}... | collective-permute-start | bytes 196616 | tf_op jit(solution)/shard_map/ppermute | solution.py:28
  41.4 5.5 %collective-permute-start.1 = (bf16[256,2,128]{2,0,1:T(8,128)(2,1)S(1)}, bf16[256,2,128]{2,0,1:T(8,128)(2,1)S(1)}, u32[]{:S(2)}, u32[]{:S(2)}) collective-permute-start(bf16[256,2,128]{2,0,1:T(8,128)(2,1)S(1)} %pad_maximum_fusion.1), channel_id=1, source_target_pairs={{0,12},{2,14},{4,0},{6,2},{8,4},{10,6},{12,8},{14,10},{1,13},{3,15... | collective-permute-start | bytes 393224 | tf_op jit(solution)/shard_map/ppermute | solution.py:28
  46.9 10.1 %collective-permute-start.2 = (bf16[512,2,128]{2,0,1:T(8,128)(2,1)S(1)}, bf16[512,2,128]{2,0,1:T(8,128)(2,1)S(1)}, u32[]{:S(2)}, u32[]{:S(2)}) collective-permute-start(bf16[512,2,128]{2,0,1:T(8,128)(2,1)S(1)} %pad_maximum_fusion), channel_id=1, source_target_pairs={{0,8},{2,10},{4,12},{6,14},{8,0},{10,2},{12,4},{14,6},{1,9},{3,11}... | collective-permute-start | bytes 786440 | tf_op jit(solution)/shard_map/ppermute | solution.py:28
  63.8 3.8 %copy-start = (f32[2,512,128,8]{2,1,3,0:T(8,128)S(1)}, f32[2,512,128,8]{2,1,3,0:T(8,128)}, u32[]{:S(2)}) copy-start(f32[2,512,128,8]{2,1,3,0:T(8,128)} %get-tuple-element.407) | copy-start | bytes 12582916 | tf_op jit(solution)/shard_map/cond/branch_1_fun/while
  73.3 4.5 %copy-start = (f32[2,512,128,8]{2,1,3,0:T(8,128)S(1)}, f32[2,512,128,8]{2,1,3,0:T(8,128)}, u32[]{:S(2)}) copy-start(f32[2,512,128,8]{2,1,3,0:T(8,128)} %get-tuple-element.407) | copy-start | bytes 12582916 | tf_op jit(solution)/shard_map/cond/branch_1_fun/while
